TPU v7x, 32 devices: a whole 2x2x4 slice. The times are simulated.
32 devices in a mesh: ulysses: 4 (over x, core), context: 8 (over z, y).
Axes of the slice: x: 2, y: 2, z: 4, core: 2. Of those that a mesh axis runs over, the one named last changes fastest.
Arguments:
- queries: bfloat16 [4096, 2048], P(('context', 'ulysses')), may hold values from -6 to 6
- key_rows: bfloat16 [4096, 2048], P(('context', 'ulysses')), may hold values from -6 to 6
- value_rows: bfloat16 [4096, 2048], P(('context', 'ulysses')), may hold values from -6 to 6
- grad_out: bfloat16 [4096, 2048], P(('context', 'ulysses')), may hold values from -6 to 6
Outputs:
- attended: bfloat16 [4096, 2048], P(('context', 'ulysses'))
- grad_queries: bfloat16 [4096, 2048], P(('context', 'ulysses'))
- grad_keys: bfloat16 [4096, 2048], P(('context', 'ulysses'))
- grad_values: bfloat16 [4096, 2048], P(('context', 'ulysses'))
All inputs are finite; a program needn't handle non-finite values.
Results may differ from a plain program's by a relative error of at most 0.03.
Values may be sent and summed in bfloat16 or wider, within the bound.
No kernel may reach another device: no remote copies, remote signals or barrier semaphores. Data moves between devices by JAX's collectives and lax.ppermute only.
A program may use at most 128 MiB of HBM per device.

v0:
```python
import jax
import jax.numpy as jnp
from jax import lax
from jax.sharding import PartitionSpec as P

HEAD_DIM = 128


def swapped(x, axis, distance):
    return lax.ppermute(x, axis, [(i, i ^ 1 << distance) for i in range(lax.axis_size(axis))])


def split_heads(flat_rows):
    return flat_rows.reshape(flat_rows.shape[0], flat_rows.shape[1] // HEAD_DIM, HEAD_DIM)


def join_heads(head_rows):
    return head_rows.reshape(head_rows.shape[0], head_rows.shape[1] * head_rows.shape[2])


def block_forward(query3, key3, value3):
    softmax_scale = HEAD_DIM ** (-0.5)
    logit_scores = (
        jnp.einsum("qhd,khd->hqk", query3, key3, preferred_element_type=jnp.float32) * softmax_scale
    )
    row_peak = jnp.max(logit_scores, axis=-1)
    shifted = jnp.exp(logit_scores - row_peak[:, :, None])
    row_total = jnp.sum(shifted, axis=-1)
    partial_out = jnp.einsum(
        "hqk,khd->qhd", shifted.astype(jnp.bfloat16), value3, preferred_element_type=jnp.float32
    )
    return (row_peak, row_total, partial_out)


def merge_block(running, fresh):
    run_peak, run_total, run_out = running
    new_peak, new_total, new_out = fresh
    joined_peak = jnp.maximum(run_peak, new_peak)
    old_factor = jnp.exp(run_peak - joined_peak)
    new_factor = jnp.exp(new_peak - joined_peak)
    joined_total = old_factor * run_total + new_factor * new_total
    joined_out = run_out * old_factor.T[:, :, None] + new_out * new_factor.T[:, :, None]
    return (joined_peak, joined_total, joined_out)


def block_backward(query3, grad3, key3, value3, log_norm, dot_term):
    softmax_scale = HEAD_DIM ** (-0.5)
    logit_scores = (
        jnp.einsum("qhd,khd->hqk", query3, key3, preferred_element_type=jnp.float32) * softmax_scale
    )
    probs = jnp.exp(logit_scores - log_norm[:, :, None])
    value_term = jnp.einsum(
        "hqk,qhd->khd", probs.astype(jnp.bfloat16), grad3, preferred_element_type=jnp.float32
    ).astype(jnp.bfloat16)
    probability_gradient = jnp.einsum(
        "qhd,khd->hqk", grad3, value3, preferred_element_type=jnp.float32
    )
    score_gradient = (probs * (probability_gradient - dot_term[:, :, None]) * softmax_scale).astype(
        jnp.bfloat16
    )
    query_term = jnp.einsum(
        "hqk,khd->qhd", score_gradient, key3, preferred_element_type=jnp.float32
    ).astype(jnp.bfloat16)
    key_term = jnp.einsum(
        "hqk,qhd->khd", score_gradient, query3, preferred_element_type=jnp.float32
    ).astype(jnp.bfloat16)
    return (query_term, key_term, value_term)


def body(queries, key_rows, value_rows, grad_out):
    levels = lax.axis_size("context").bit_length() - 1
    query_flat, key_flat, value_flat, grad_flat = (
        lax.all_to_all(queries, "ulysses", split_axis=1, concat_axis=0, tiled=True),
        lax.all_to_all(key_rows, "ulysses", split_axis=1, concat_axis=0, tiled=True),
        lax.all_to_all(value_rows, "ulysses", split_axis=1, concat_axis=0, tiled=True),
        lax.all_to_all(grad_out, "ulysses", split_axis=1, concat_axis=0, tiled=True),
    )
    query3 = split_heads(query_flat)
    key3 = split_heads(key_flat)
    value3 = split_heads(value_flat)
    grad3 = split_heads(grad_flat)
    running = block_forward(query3, key3, value3)
    cached = []
    for level in range(levels):
        remote_key, remote_value = swapped((key_flat, value_flat), "context", level)
        cached.append((remote_key, remote_value))
        running = merge_block(
            running, block_forward(query3, split_heads(remote_key), split_heads(remote_value))
        )
    run_peak, run_total, run_out = running
    output3 = (run_out / run_total.T[:, :, None]).astype(jnp.bfloat16)
    log_norm = run_peak + jnp.log(run_total)
    dot_term = jnp.sum(grad3.astype(jnp.float32) * output3.astype(jnp.float32), axis=-1).T
    own_terms = block_backward(query3, grad3, key3, value3, log_norm, dot_term)
    grad_query = own_terms[0].astype(jnp.float32)
    grad_key = own_terms[1].astype(jnp.float32)
    grad_value = own_terms[2].astype(jnp.float32)
    for level in range(levels):
        remote_key, remote_value = swapped((key_flat, value_flat), "context", level)
        terms = block_backward(
            query3, grad3, split_heads(remote_key), split_heads(remote_value), log_norm, dot_term
        )
        grad_query = grad_query + terms[0].astype(jnp.float32)
        outgoing = (terms[1], terms[2])
        returned = swapped((outgoing[0], outgoing[1]), "context", level)
        grad_key = grad_key + returned[0].astype(jnp.float32)
        grad_value = grad_value + returned[1].astype(jnp.float32)
    results = (
        lax.all_to_all(join_heads(output3), "ulysses", split_axis=0, concat_axis=1, tiled=True),
        lax.all_to_all(
            join_heads(grad_query.astype(jnp.bfloat16)),
            "ulysses",
            split_axis=0,
            concat_axis=1,
            tiled=True,
        ),
        lax.all_to_all(
            join_heads(grad_key.astype(jnp.bfloat16)),
            "ulysses",
            split_axis=0,
            concat_axis=1,
            tiled=True,
        ),
        lax.all_to_all(
            join_heads(grad_value.astype(jnp.bfloat16)),
            "ulysses",
            split_axis=0,
            concat_axis=1,
            tiled=True,
        ),
    )
    return (results[0], results[1], results[2], results[3])


def solution(mesh):
    placed = (
        P(("context", "ulysses"), None),
        P(("context", "ulysses"), None),
        P(("context", "ulysses"), None),
        P(("context", "ulysses"), None),
    )
    return jax.shard_map(
        body,
        mesh=mesh,
        in_specs=placed,
        out_specs=(
            P(("context", "ulysses"), None),
            P(("context", "ulysses"), None),
            P(("context", "ulysses"), None),
            P(("context", "ulysses"), None),
        ),
        check_vma=False,
    )
```

profile of v0, /device:TPU:0, one launch (start us, length us, event | category | flops | bytes accessed | tf_op | source)
XLA Modules:
  0.0 214.5 jit_solution(4984784563907744337)
XLA Ops:
  0.7 2.0 copy.337
  2.6 4.2 %all-to-all-start = ((bf16[128,4,512]{2,0,1:T(8,128)(2,1)}), bf16[128,4,512]{2,0,1:T(8,128)(2,1)S(1)}, u32[]{:S(2)}, u32[]{:S(2)}) async-start(bf16[128,4,512]{2,0,1:T(8,128)(2,1)} %bitcast.183), calls=%async_computation | async-start | bytes 1048576 | tf_op jit(solution)/shard_map/all_to_all | solution.py:73
  6.9 2.0 copy.207
  8.9 6.8 %all-to-all-done = bf16[128,4,512]{2,0,1:T(8,128)(2,1)S(1)} async-done(((bf16[128,4,512]{2,0,1:T(8,128)(2,1)}), bf16[128,4,512]{2,0,1:T(8,128)(2,1)S(1)}, u32[]{:S(2)}, u32[]{:S(2)}) %all-to-all-start) | async-done | bytes 524320 | tf_op jit(solution)/shard_map/all_to_all | solution.py:73
  15.7 3.5 %all-to-all-start.1 = ((bf16[128,4,512]{0,2,1:T(8,128)(2,1)}), bf16[128,4,512]{0,2,1:T(8,128)(2,1)S(1)}, u32[]{:S(2)}, u32[]{:S(2)}) async-start(bf16[128,4,512]{0,2,1:T(8,128)(2,1)} %bitcast.1), calls=%async_computation.1 | async-start | bytes 1048576 | tf_op jit(solution)/shard_map/all_to_all | solution.py:74
  20.2 7.8 %all-to-all-done.1 = bf16[128,4,512]{0,2,1:T(8,128)(2,1)S(1)} async-done(((bf16[128,4,512]{0,2,1:T(8,128)(2,1)}), bf16[128,4,512]{0,2,1:T(8,128)(2,1)S(1)}, u32[]{:S(2)}, u32[]{:S(2)}) %all-to-all-start.1) | async-done | bytes 524320 | tf_op jit(solution)/shard_map/all_to_all | solution.py:74
  27.9 3.5 %all-to-all-start.2 = ((bf16[128,4,512]{0,2,1:T(8,128)(2,1)}), bf16[128,4,512]{0,2,1:T(8,128)(2,1)S(1)}, u32[]{:S(2)}, u32[]{:S(2)}) async-start(bf16[128,4,512]{0,2,1:T(8,128)(2,1)} %bitcast.3), calls=%async_computation.2 | async-start | bytes 1048576 | tf_op jit(solution)/shard_map/all_to_all | solution.py:75
  31.6 2.3 %collective-permute-start = (bf16[512,512]{1,0:T(8,128)(2,1)S(1)}, bf16[512,512]{1,0:T(8,128)(2,1)}, u32[]{:S(2)}, u32[]{:S(2)}) collective-permute-start(bf16[512,512]{1,0:T(8,128)(2,1)S(1)} %bitcast.197), channel_id=1, source_target_pairs={{0,1},{1,0},{2,3},{3,2},{4,5},{5,4},{6,7},{7,6},{8,9},{9,8},{10,11... | collective-permute-start | bytes 1572872 | tf_op jit(solution)/shard_map/ppermute | solution.py:10
  34.9 5.3 %all-to-all-done.2 = bf16[128,4,512]{0,2,1:T(8,128)(2,1)S(1)} async-done(((bf16[128,4,512]{0,2,1:T(8,128)(2,1)}), bf16[128,4,512]{0,2,1:T(8,128)(2,1)S(1)}, u32[]{:S(2)}, u32[]{:S(2)}) %all-to-all-start.2) | async-done | bytes 524320 | tf_op jit(solution)/shard_map/all_to_all | solution.py:75
  40.2 3.5 %all-to-all-start.4 = ((bf16[128,4,512]{0,2,1:T(8,128)(2,1)}), bf16[128,4,512]{0,2,1:T(8,128)(2,1)S(1)}, u32[]{:S(2)}, u32[]{:S(2)}) async-start(bf16[128,4,512]{0,2,1:T(8,128)(2,1)} %bitcast.29), calls=%async_computation.4 | async-start | bytes 1048576 | tf_op jit(solution)/shard_map/all_to_all | solution.py:76
  44.8 3.3 %collective-permute-start.5 = (bf16[512,512]{1,0:T(8,128)(2,1)}, bf16[512,512]{1,0:T(8,128)(2,1)}, u32[]{:S(2)}, u32[]{:S(2)}) collective-permute-start(bf16[512,512]{1,0:T(8,128)(2,1)} %bitcast.11), channel_id=1, source_target_pairs={{0,4},{1,5},{2,6},{3,7},{4,0},{5,1},{6,2},{7,3},{8,12},{9,13},{10,... | collective-permute-start | bytes 1572872 | tf_op jit(solution)/shard_map/ppermute | solution.py:10
  48.1 1.6 collective-permute-start.3
  49.7 1.5 collective-permute-start.1
  51.8 2.7 %multiply_reduce_fusion.3 = (f32[4,512]{1,0:T(4,128)S(1)}, f32[4,512,512]{1,2,0:T(8,128)}) fusion(bf16[512,4,128]{2,1,0:T(4,128)(2,1)S(1)} %reshape.135, bf16[512,4,128]{2,1,0:T(4,128)(2,1)S(1)} %reshape.134), kind=kOutput, calls=%fused_computation.27 | convolution fusion | flops 270530560 | bytes 5251072 | tf_op jit(solution)/shard_map/qhd,khd->hqk/dot_general | solution.py:24
  54.4 1.2 copy.213
  55.7 1.2 reshape.136
  57.9 1.3 copy.216
  59.2 2.8 %multiply_reduce_fusion.2 = (f32[4,512]{1,0:T(4,128)S(1)}, f32[4,512,512]{1,2,0:T(8,128)}) fusion(bf16[512,4,128]{0,2,1:T(8,128)(2,1)S(1)} %bitcast.184, bf16[512,4,128]{2,1,0:T(4,128)(2,1)S(1)} %reshape.134), kind=kOutput, calls=%fused_computation.26 | convolution fusion | flops 270530560 | bytes 5251072 | tf_op jit(solution)/shard_map/qhd,khd->hqk/dot_general | solution.py:24
  62.0 33.0 %collective-permute-done.2 = bf16[512,512]{1,0:T(8,128)(2,1)} collective-permute-done((bf16[512,512]{1,0:T(8,128)(2,1)S(1)}, bf16[512,512]{1,0:T(8,128)(2,1)}, u32[]{:S(2)}, u32[]{:S(2)}) %collective-permute-start.2) | collective-permute-done | bytes 524320 | tf_op jit(solution)/shard_map/ppermute | solution.py:10
  95.0 1.3 copy.221
  96.2 2.8 %multiply_reduce_fusion.1 = (f32[4,512]{1,0:T(4,128)S(1)}, f32[4,512,512]{1,2,0:T(8,128)}) fusion(bf16[512,4,128]{0,2,1:T(8,128)(2,1)S(1)} %bitcast.186, bf16[512,4,128]{2,1,0:T(4,128)(2,1)S(1)} %reshape.134), kind=kOutput, calls=%fused_computation.25 | convolution fusion | flops 270530560 | bytes 5251072 | tf_op jit(solution)/shard_map/qhd,khd->hqk/dot_general | solution.py:24
  99.0 1.3 copy.226
  101.1 3.1 %copy-done.2 = f32[4,512,512]{1,2,0:T(8,128)S(1)} copy-done((f32[4,512,512]{1,2,0:T(8,128)S(1)}, f32[4,512,512]{1,2,0:T(8,128)}, u32[]{:S(2)}) %copy-start.2) | copy-done | bytes 4194328
  104.2 1.4 fusion.4
  106.3 1.3 copy-done.8
  107.6 1.4 fusion
  109.1 1.6 fusion.121
  110.7 1.9 fusion.47
  112.6 1.3 copy.224
  113.9 4.2 %fusion.74 = f32[512,4,128]{0,2,1:T(8,128)} fusion(bf16[512,4,128]{0,2,1:T(8,128)(2,1)S(1)} %bitcast.190, f32[4,512,512]{1,2,0:T(8,128)} %get-tuple-element.26, f32[4,512]{1,0:T(4,128)S(1)} %get-tuple-element.25, f32[512,4]{0,1:T(4,128)S(1)} %get-tuple-element.21), kind=kOutput, calls=%fused_computation.62 | convolution fusion | flops 271843328 | bytes 5783552 | tf_op jit(solution)/shard_map/hqk,khd->qhd/dot_general | solution.py:29
  118.2 1.8 fusion.118
  120.0 1.6 fusion.115
  121.6 1.3 copy.229
  122.9 4.1 %fusion.80 = f32[512,4,128]{0,2,1:T(8,128)} fusion(bf16[512,4,128]{0,2,1:T(8,128)(2,1)S(1)} %bitcast.192, f32[4,512,512]{1,2,0:T(8,128)} %copy-done.5, f32[4,512]{1,0:T(4,128)S(1)} %get-tuple-element.23, f32[512,4]{0,1:T(4,128)S(1)} %get-tuple-element.22), kind=kOutput, calls=%fused_computation.64 | convolution fusion | flops 271843328 | bytes 5783552 | tf_op jit(solution)/shard_map/hqk,khd->qhd/dot_general | solution.py:29
  127.0 1.3 copy.219
  128.3 5.2 %multiply_reduce_fusion.4 = (f32[512,4]{0,1:T(4,128)S(1)}, bf16[512,4,128]{0,2,1:T(8,128)(2,1)}) fusion(bf16[512,4,128]{0,2,1:T(8,128)(2,1)S(1)} %reshape.143, f32[512,4]{0,1:T(4,128)S(1)} %get-tuple-element.16, f32[512,4,128]{0,2,1:T(8,128)} %fusion.80, f32[512,4]{0,1:T(4,128)S(1)} %get-tuple-element.19, f32[512,4,128]{0,2,1:T(8,128)} %fusion.74, ...), kind=kOutput, calls=%fused_computation.98 | convolution fusion | flops 274724864 | bytes 8962048 | tf_op jit(solution)/shard_map/hqk,khd->qhd/dot_general | solution.py:29
  133.4 1.4 multiply_convert_fusion.2
  135.6 1.4 multiply_convert_fusion.1
  137.1 1.5 copy-done.7
  138.6 1.4 multiply_convert_fusion
  140.0 1.5 copy-done.1
  141.6 1.4 multiply_convert_fusion.3
  143.1 1.5 fusion.114
  146.1 2.6 %collective-permute-start.10 = (bf16[512,4,128]{2,0,1:T(8,128)(2,1)}, bf16[512,4,128]{2,0,1:T(8,128)(2,1)}, u32[]{:S(2)}, u32[]{:S(2)}) collective-permute-start(bf16[512,4,128]{2,0,1:T(8,128)(2,1)} %fusion.118), channel_id=1, source_target_pairs={{0,2},{1,3},{2,0},{3,1},{4,6},{5,7},{6,4},{7,5},{8,10},{9,11},{10,... | collective-permute-start | bytes 1572872 | tf_op jit(solution)/shard_map/ppermute | solution.py:10
  148.7 1.5 collective-permute-start.9
  152.1 1.2 fusion.111
  153.3 1.2 copy.254
  154.5 2.0 all_to_all.126
  156.5 4.1 %all-to-all-start.5 = ((bf16[4,128,512]{2,1,0:T(8,128)(2,1)}), bf16[4,128,512]{2,1,0:T(8,128)(2,1)}, u32[]{:S(2)}, u32[]{:S(2)}) async-start(bf16[4,128,512]{2,1,0:T(8,128)(2,1)} %all_to_all.126), calls=%async_computation.5 | async-start | bytes 1048576 | tf_op jit(solution)/shard_map/all_to_all | solution.py:110
  160.6 3.1 %fusion.112 = bf16[512,4,128]{2,0,1:T(8,128)(2,1)} fusion(bf16[4,512,512]{1,2,0:T(8,128)(2,1)} %copy-done.11, bf16[512,4,128]{2,1,0:T(4,128)(2,1)S(1)} %reshape.134), kind=kOutput, calls=%fused_computation.90 | convolution fusion | flops 268697600 | bytes 3145728 | tf_op jit(solution)/shard_map/hqk,qhd->khd/dot_general | solution.py:64
  164.3 3.1 %fusion.113 = bf16[512,4,128]{2,0,1:T(8,128)(2,1)} fusion(bf16[4,512,512]{1,2,0:T(8,128)(2,1)} %copy-done.10, bf16[512,4,128]{2,1,0:T(4,128)(2,1)S(1)} %reshape.134), kind=kOutput, calls=%fused_computation.91 | convolution fusion | flops 268697600 | bytes 3145728 | tf_op jit(solution)/shard_map/hqk,qhd->khd/dot_general | solution.py:64
  167.4 3.8 %collective-permute-done.11 = bf16[512,4,128]{2,0,1:T(8,128)(2,1)} collective-permute-done((bf16[512,4,128]{2,0,1:T(8,128)(2,1)}, bf16[512,4,128]{2,0,1:T(8,128)(2,1)}, u32[]{:S(2)}, u32[]{:S(2)}) %collective-permute-start.11) | collective-permute-done | bytes 524320 | tf_op jit(solution)/shard_map/ppermute | solution.py:10
  171.2 2.0 all_to_all.119
  173.2 1.9 copy.231
  175.1 4.1 %all-to-all-start.3 = ((bf16[4,128,512]{1,2,0:T(8,128)(2,1)}), bf16[4,128,512]{1,2,0:T(8,128)(2,1)}, u32[]{:S(2)}, u32[]{:S(2)}) async-start(bf16[4,128,512]{1,2,0:T(8,128)(2,1)} %copy.231), calls=%async_computation.3 | async-start | bytes 1048576 | tf_op jit(solution)/shard_map/all_to_all | solution.py:109
  179.2 3.6 %add_convert_fusion = bf16[512,4,128]{2,0,1:T(8,128)(2,1)S(1)} fusion(bf16[512,4,128]{2,0,1:T(8,128)(2,1)} %collective-permute-done.11, bf16[512,4,128]{2,0,1:T(8,128)(2,1)} %collective-permute-done.10, bf16[512,4,128]{2,0,1:T(8,128)(2,1)} %collective-permute-done.9, bf16[512,4,128]{0,2,1:T(8,128)(2,1)S(1)} %reshape.143, ...), kind=kOutput, calls=%fused_computation.96 | convolution fusion | flops 273940480 | bytes 6823936 | tf_op jit(solution)/shard_map/hqk,qhd->khd/dot_general | solution.py:52
  184.3 3.8 %all-to-all-done.3 = bf16[4,128,512]{1,2,0:T(8,128)(2,1)} async-done(((bf16[4,128,512]{1,2,0:T(8,128)(2,1)}), bf16[4,128,512]{1,2,0:T(8,128)(2,1)}, u32[]{:S(2)}, u32[]{:S(2)}) %all-to-all-start.3) | async-done | bytes 524320 | tf_op jit(solution)/shard_map/all_to_all | solution.py:109
  188.1 3.5 %all-to-all-start.7 = ((bf16[4,128,512]{2,1,0:T(8,128)(2,1)}), bf16[4,128,512]{2,1,0:T(8,128)(2,1)S(1)}, u32[]{:S(2)}, u32[]{:S(2)}) async-start(bf16[4,128,512]{2,1,0:T(8,128)(2,1)} %all_to_all.134), calls=%async_computation.7 | async-start | bytes 1048576 | tf_op jit(solution)/shard_map/all_to_all | solution.py:124
  191.6 5.9 %collective-permute-done.8 = bf16[512,4,128]{2,0,1:T(8,128)(2,1)} collective-permute-done((bf16[512,4,128]{2,0,1:T(8,128)(2,1)}, bf16[512,4,128]{2,0,1:T(8,128)(2,1)}, u32[]{:S(2)}, u32[]{:S(2)}) %collective-permute-start.8) | collective-permute-done | bytes 524320 | tf_op jit(solution)/shard_map/ppermute | solution.py:10
  197.5 2.1 add_convert_fusion.1
  201.0 3.5 %all-to-all-start.6 = ((bf16[4,128,512]{2,1,0:T(8,128)(2,1)}), bf16[4,128,512]{2,1,0:T(8,128)(2,1)S(1)}, u32[]{:S(2)}, u32[]{:S(2)}) async-start(bf16[4,128,512]{2,1,0:T(8,128)(2,1)} %all_to_all.130), calls=%async_computation.6 | async-start | bytes 1048576 | tf_op jit(solution)/shard_map/all_to_all | solution.py:117
  204.4 1.3 copy.255
  206.8 2.0 copy.268
  210.1 3.1 %all-to-all-done.6 = bf16[4,128,512]{2,1,0:T(8,128)(2,1)S(1)} async-done(((bf16[4,128,512]{2,1,0:T(8,128)(2,1)}), bf16[4,128,512]{2,1,0:T(8,128)(2,1)S(1)}, u32[]{:S(2)}, u32[]{:S(2)}) %all-to-all-start.6) | async-done | bytes 524320 | tf_op jit(solution)/shard_map/all_to_all | solution.py:117
  (85 shorter events, 17.7 us)
Async XLA Ops:
  0.6 18.5 %copy-start.22 = (bf16[128,2048]{1,0:T(8,128)(2,1)S(1)}, bf16[128,2048]{1,0:T(8,128)(2,1)}, u32[]{:S(2)}) copy-start(bf16[128,2048]{1,0:T(8,128)(2,1)} %param.6) | copy-start | bytes 1572868
  0.6 33.3 %copy-start.23 = (bf16[128,2048]{1,0:T(8,128)(2,1)S(1)}, bf16[128,2048]{1,0:T(8,128)(2,1)}, u32[]{:S(2)}) copy-start(bf16[128,2048]{1,0:T(8,128)(2,1)} %param.7) | copy-start | bytes 1572868
  2.6 13.1 %all-to-all-start = ((bf16[128,4,512]{2,0,1:T(8,128)(2,1)}), bf16[128,4,512]{2,0,1:T(8,128)(2,1)S(1)}, u32[]{:S(2)}, u32[]{:S(2)}) async-start(bf16[128,4,512]{2,0,1:T(8,128)(2,1)} %bitcast.183), calls=%async_computation | async-start | bytes 1048576 | tf_op jit(solution)/shard_map/all_to_all | solution.py:73
  15.7 12.3 %all-to-all-start.1 = ((bf16[128,4,512]{0,2,1:T(8,128)(2,1)}), bf16[128,4,512]{0,2,1:T(8,128)(2,1)S(1)}, u32[]{:S(2)}, u32[]{:S(2)}) async-start(bf16[128,4,512]{0,2,1:T(8,128)(2,1)} %bitcast.1), calls=%async_computation.1 | async-start | bytes 1048576 | tf_op jit(solution)/shard_map/all_to_all | solution.py:74
  27.9 12.3 %all-to-all-start.2 = ((bf16[128,4,512]{0,2,1:T(8,128)(2,1)}), bf16[128,4,512]{0,2,1:T(8,128)(2,1)S(1)}, u32[]{:S(2)}, u32[]{:S(2)}) async-start(bf16[128,4,512]{0,2,1:T(8,128)(2,1)} %bitcast.3), calls=%async_computation.2 | async-start | bytes 1048576 | tf_op jit(solution)/shard_map/all_to_all | solution.py:75
  31.6 25.9 %collective-permute-start = (bf16[512,512]{1,0:T(8,128)(2,1)S(1)}, bf16[512,512]{1,0:T(8,128)(2,1)}, u32[]{:S(2)}, u32[]{:S(2)}) collective-permute-start(bf16[512,512]{1,0:T(8,128)(2,1)S(1)} %bitcast.197), channel_id=1, source_target_pairs={{0,1},{1,0},{2,3},{3,2},{4,5},{5,4},{6,7},{7,6},{8,9},{9,8},{10,11... | collective-permute-start | bytes 1572872 | tf_op jit(solution)/shard_map/ppermute | solution.py:10
  40.2 16.7 %all-to-all-start.4 = ((bf16[128,4,512]{0,2,1:T(8,128)(2,1)}), bf16[128,4,512]{0,2,1:T(8,128)(2,1)S(1)}, u32[]{:S(2)}, u32[]{:S(2)}) async-start(bf16[128,4,512]{0,2,1:T(8,128)(2,1)} %bitcast.29), calls=%async_computation.4 | async-start | bytes 1048576 | tf_op jit(solution)/shard_map/all_to_all | solution.py:76
  43.8 11.9 %copy-start.12 = (bf16[512,4,128]{2,1,0:T(4,128)(2,1)}, bf16[512,4,128]{2,1,0:T(4,128)(2,1)S(1)}, u32[]{:S(2)}) copy-start(bf16[512,4,128]{2,1,0:T(4,128)(2,1)S(1)} %reshape.135) | copy-start | bytes 1572868
  44.8 76.8 %collective-permute-start.5 = (bf16[512,512]{1,0:T(8,128)(2,1)}, bf16[512,512]{1,0:T(8,128)(2,1)}, u32[]{:S(2)}, u32[]{:S(2)}) collective-permute-start(bf16[512,512]{1,0:T(8,128)(2,1)} %bitcast.11), channel_id=1, source_target_pairs={{0,4},{1,5},{2,6},{3,7},{4,0},{5,1},{6,2},{7,3},{8,12},{9,13},{10,... | collective-permute-start | bytes 1572872 | tf_op jit(solution)/shard_map/ppermute | solution.py:10
  48.1 64.5 %collective-permute-start.3 = (bf16[512,512]{1,0:T(8,128)(2,1)}, bf16[512,512]{1,0:T(8,128)(2,1)}, u32[]{:S(2)}, u32[]{:S(2)}) collective-permute-start(bf16[512,512]{1,0:T(8,128)(2,1)} %bitcast.11), channel_id=1, source_target_pairs={{0,2},{1,3},{2,0},{3,1},{4,6},{5,7},{6,4},{7,5},{8,10},{9,11},{10,... | collective-permute-start | bytes 1572872 | tf_op jit(solution)/shard_map/ppermute | solution.py:10
  49.7 77.3 %collective-permute-start.1 = (bf16[512,512]{1,0:T(8,128)(2,1)}, bf16[512,512]{1,0:T(8,128)(2,1)}, u32[]{:S(2)}, u32[]{:S(2)}) collective-permute-start(bf16[512,512]{1,0:T(8,128)(2,1)} %bitcast.11), channel_id=1, source_target_pairs={{0,1},{1,0},{2,3},{3,2},{4,5},{5,4},{6,7},{7,6},{8,9},{9,8},{10,11... | collective-permute-start | bytes 1572872 | tf_op jit(solution)/shard_map/ppermute | solution.py:10
  51.2 43.8 %collective-permute-start.2 = (bf16[512,512]{1,0:T(8,128)(2,1)S(1)}, bf16[512,512]{1,0:T(8,128)(2,1)}, u32[]{:S(2)}, u32[]{:S(2)}) collective-permute-start(bf16[512,512]{1,0:T(8,128)(2,1)S(1)} %bitcast.198), channel_id=1, source_target_pairs={{0,2},{1,3},{2,0},{3,1},{4,6},{5,7},{6,4},{7,5},{8,10},{9,11},{10,... | collective-permute-start | bytes 1572872 | tf_op jit(solution)/shard_map/ppermute | solution.py:10
  56.9 53.8 %copy-start.16 = (bf16[512,4,128]{0,2,1:T(8,128)(2,1)}, bf16[512,4,128]{0,2,1:T(8,128)(2,1)S(1)}, u32[]{:S(2)}) copy-start(bf16[512,4,128]{0,2,1:T(8,128)(2,1)S(1)} %reshape.136) | copy-start | bytes 1572868
  57.5 41.5 %collective-permute-start.4 = (bf16[512,512]{1,0:T(8,128)(2,1)S(1)}, bf16[512,512]{1,0:T(8,128)(2,1)}, u32[]{:S(2)}, u32[]{:S(2)}) collective-permute-start(bf16[512,512]{1,0:T(8,128)(2,1)S(1)} %bitcast.199), channel_id=1, source_target_pairs={{0,4},{1,5},{2,6},{3,7},{4,0},{5,1},{6,2},{7,3},{8,12},{9,13},{10,... | collective-permute-start | bytes 1572872 | tf_op jit(solution)/shard_map/ppermute | solution.py:10
  59.2 39.8 %copy-start.14 = (bf16[512,512]{0,1:T(8,128)(2,1)}, bf16[512,512]{0,1:T(8,128)(2,1)S(1)}, u32[]{:S(2)}) copy-start(bf16[512,512]{0,1:T(8,128)(2,1)S(1)} %copy.216) | copy-start | bytes 1572868
  96.2 4.8 %copy-start.18 = (bf16[512,512]{0,1:T(8,128)(2,1)}, bf16[512,512]{0,1:T(8,128)(2,1)S(1)}, u32[]{:S(2)}) copy-start(bf16[512,512]{0,1:T(8,128)(2,1)S(1)} %copy.221) | copy-start | bytes 1572868
  100.3 5.3 %copy-start.20 = (bf16[512,512]{0,1:T(8,128)(2,1)}, bf16[512,512]{0,1:T(8,128)(2,1)S(1)}, u32[]{:S(2)}) copy-start(bf16[512,512]{0,1:T(8,128)(2,1)S(1)} %copy.226) | copy-start | bytes 1572868
  100.3 3.9 %copy-start.2 = (f32[4,512,512]{1,2,0:T(8,128)S(1)}, f32[4,512,512]{1,2,0:T(8,128)}, u32[]{:S(2)}) copy-start(f32[4,512,512]{1,2,0:T(8,128)} %get-tuple-element.26) | copy-start | bytes 12582916
  101.1 4.5 %copy-start.5 = (f32[4,512,512]{1,2,0:T(8,128)}, f32[4,512,512]{1,2,0:T(8,128)S(1)}, u32[]{:S(2)}) copy-start(f32[4,512,512]{1,2,0:T(8,128)S(1)} %get-tuple-element.24) | copy-start | bytes 12582916
  104.2 2.2 %copy-start = (f32[4,512,512]{1,2,0:T(8,128)S(1)}, f32[4,512,512]{1,2,0:T(8,128)}, u32[]{:S(2)}) copy-start(f32[4,512,512]{1,2,0:T(8,128)} %get-tuple-element.30) | copy-start | bytes 12582916
  104.2 3.5 %copy-start.8 = (f32[4,512,512]{1,2,0:T(8,128)S(1)}, f32[4,512,512]{1,2,0:T(8,128)}, u32[]{:S(2)}) copy-start(f32[4,512,512]{1,2,0:T(8,128)} %get-tuple-element.28) | copy-start | bytes 12582916
  113.9 4.3 %copy-start.3 = (f32[4,512,512]{1,2,0:T(8,128)S(1)}, f32[4,512,512]{1,2,0:T(8,128)}, u32[]{:S(2)}) copy-start(f32[4,512,512]{1,2,0:T(8,128)} %get-tuple-element.26) | copy-start | bytes 12582916
  113.9 6.1 %copy-start.6 = (f32[4,512,512]{1,2,0:T(8,128)S(1)}, f32[4,512,512]{1,2,0:T(8,128)}, u32[]{:S(2)}) copy-start(f32[4,512,512]{1,2,0:T(8,128)} %copy-done.5) | copy-start | bytes 12582916
  128.2 5.2 %copy-start.9 = (f32[4,512,512]{1,2,0:T(8,128)S(1)}, f32[4,512,512]{1,2,0:T(8,128)}, u32[]{:S(2)}) copy-start(f32[4,512,512]{1,2,0:T(8,128)} %get-tuple-element.28) | copy-start | bytes 12582916
  133.4 2.2 %copy-start.4 = (f32[4,512,512]{1,2,0:T(8,128)S(1)}, f32[4,512,512]{1,2,0:T(8,128)}, u32[]{:S(2)}) copy-start(f32[4,512,512]{1,2,0:T(8,128)} %get-tuple-element.26) | copy-start | bytes 12582916
  135.6 16.5 %copy-start.11 = (bf16[4,512,512]{1,2,0:T(8,128)(2,1)}, bf16[4,512,512]{1,2,0:T(8,128)(2,1)S(1)}, u32[]{:S(2)}) copy-start(bf16[4,512,512]{1,2,0:T(8,128)(2,1)S(1)} %multiply_convert_fusion.2) | copy-start | bytes 6291460
  135.6 2.9 %copy-start.7 = (f32[4,512,512]{1,2,0:T(8,128)S(1)}, f32[4,512,512]{1,2,0:T(8,128)}, u32[]{:S(2)}) copy-start(f32[4,512,512]{1,2,0:T(8,128)} %copy-done.5) | copy-start | bytes 12582916
  138.6 12.6 %copy-start.10 = (bf16[4,512,512]{1,2,0:T(8,128)(2,1)}, bf16[4,512,512]{1,2,0:T(8,128)(2,1)S(1)}, u32[]{:S(2)}) copy-start(bf16[4,512,512]{1,2,0:T(8,128)(2,1)S(1)} %multiply_convert_fusion.1) | copy-start | bytes 6291460
  138.6 2.9 %copy-start.1 = (f32[4,512,512]{1,2,0:T(8,128)S(1)}, f32[4,512,512]{1,2,0:T(8,128)}, u32[]{:S(2)}) copy-start(f32[4,512,512]{1,2,0:T(8,128)} %get-tuple-element.30) | copy-start | bytes 12582916
  138.6 3.1 %copy-start.17 = (bf16[512,4,128]{0,2,1:T(8,128)(2,1)S(1)}, bf16[512,4,128]{0,2,1:T(8,128)(2,1)}, u32[]{:S(2)}) copy-start(bf16[512,4,128]{0,2,1:T(8,128)(2,1)} %copy-done.16) | copy-start | bytes 1572868
  141.6 3.0 %copy-start.21 = (bf16[512,512]{0,1:T(8,128)(2,1)S(1)}, bf16[512,512]{0,1:T(8,128)(2,1)}, u32[]{:S(2)}) copy-start(bf16[512,512]{0,1:T(8,128)(2,1)} %copy-done.20) | copy-start | bytes 1572868
  143.1 7.1 %copy-start.13 = (bf16[512,4,128]{2,1,0:T(4,128)(2,1)S(1)}, bf16[512,4,128]{2,1,0:T(4,128)(2,1)}, u32[]{:S(2)}) copy-start(bf16[512,4,128]{2,1,0:T(4,128)(2,1)} %copy-done.12) | copy-start | bytes 1572868
  144.6 6.5 %copy-start.19 = (bf16[512,512]{0,1:T(8,128)(2,1)S(1)}, bf16[512,512]{0,1:T(8,128)(2,1)}, u32[]{:S(2)}) copy-start(bf16[512,512]{0,1:T(8,128)(2,1)} %copy-done.18) | copy-start | bytes 1572868
  145.5 6.6 %copy-start.15 = (bf16[512,512]{0,1:T(8,128)(2,1)S(1)}, bf16[512,512]{0,1:T(8,128)(2,1)}, u32[]{:S(2)}) copy-start(bf16[512,512]{0,1:T(8,128)(2,1)} %copy-done.14) | copy-start | bytes 1572868
  145.5 25.7 %collective-permute-start.11 = (bf16[512,4,128]{2,0,1:T(8,128)(2,1)}, bf16[512,4,128]{2,0,1:T(8,128)(2,1)}, u32[]{:S(2)}, u32[]{:S(2)}) collective-permute-start(bf16[512,4,128]{2,0,1:T(8,128)(2,1)} %fusion.115), channel_id=1, source_target_pairs={{0,4},{1,5},{2,6},{3,7},{4,0},{5,1},{6,2},{7,3},{8,12},{9,13},{10,... | collective-permute-start | bytes 1572872 | tf_op jit(solution)/shard_map/ppermute | solution.py:10
  146.1 33.1 %collective-permute-start.10 = (bf16[512,4,128]{2,0,1:T(8,128)(2,1)}, bf16[512,4,128]{2,0,1:T(8,128)(2,1)}, u32[]{:S(2)}, u32[]{:S(2)}) collective-permute-start(bf16[512,4,128]{2,0,1:T(8,128)(2,1)} %fusion.118), channel_id=1, source_target_pairs={{0,2},{1,3},{2,0},{3,1},{4,6},{5,7},{6,4},{7,5},{8,10},{9,11},{10,... | collective-permute-start | bytes 1572872 | tf_op jit(solution)/shard_map/ppermute | solution.py:10
  148.7 30.5 %collective-permute-start.9 = (bf16[512,4,128]{2,0,1:T(8,128)(2,1)}, bf16[512,4,128]{2,0,1:T(8,128)(2,1)}, u32[]{:S(2)}, u32[]{:S(2)}) collective-permute-start(bf16[512,4,128]{2,0,1:T(8,128)(2,1)} %fusion.121), channel_id=1, source_target_pairs={{0,1},{1,0},{2,3},{3,2},{4,5},{5,4},{6,7},{7,6},{8,9},{9,8},{10,11... | collective-permute-start | bytes 1572872 | tf_op jit(solution)/shard_map/ppermute | solution.py:10
  156.5 18.6 %all-to-all-start.5 = ((bf16[4,128,512]{2,1,0:T(8,128)(2,1)}), bf16[4,128,512]{2,1,0:T(8,128)(2,1)}, u32[]{:S(2)}, u32[]{:S(2)}) async-start(bf16[4,128,512]{2,1,0:T(8,128)(2,1)} %all_to_all.126), calls=%async_computation.5 | async-start | bytes 1048576 | tf_op jit(solution)/shard_map/all_to_all | solution.py:110
  163.8 27.8 %collective-permute-start.6 = (bf16[512,4,128]{2,0,1:T(8,128)(2,1)}, bf16[512,4,128]{2,0,1:T(8,128)(2,1)}, u32[]{:S(2)}, u32[]{:S(2)}) collective-permute-start(bf16[512,4,128]{2,0,1:T(8,128)(2,1)} %fusion.112), channel_id=1, source_target_pairs={{0,1},{1,0},{2,3},{3,2},{4,5},{5,4},{6,7},{7,6},{8,9},{9,8},{10,11... | collective-permute-start | bytes 1572872 | tf_op jit(solution)/shard_map/ppermute | solution.py:10
  167.4 24.2 %collective-permute-start.7 = (bf16[512,4,128]{2,0,1:T(8,128)(2,1)}, bf16[512,4,128]{2,0,1:T(8,128)(2,1)}, u32[]{:S(2)}, u32[]{:S(2)}) collective-permute-start(bf16[512,4,128]{2,0,1:T(8,128)(2,1)} %fusion.113), channel_id=1, source_target_pairs={{0,2},{1,3},{2,0},{3,1},{4,6},{5,7},{6,4},{7,5},{8,10},{9,11},{10,... | collective-permute-start | bytes 1572872 | tf_op jit(solution)/shard_map/ppermute | solution.py:10
  171.2 26.3 %collective-permute-start.8 = (bf16[512,4,128]{2,0,1:T(8,128)(2,1)}, bf16[512,4,128]{2,0,1:T(8,128)(2,1)}, u32[]{:S(2)}, u32[]{:S(2)}) collective-permute-start(bf16[512,4,128]{2,0,1:T(8,128)(2,1)} %fusion.114), channel_id=1, source_target_pairs={{0,4},{1,5},{2,6},{3,7},{4,0},{5,1},{6,2},{7,3},{8,12},{9,13},{10,... | collective-permute-start | bytes 1572872 | tf_op jit(solution)/shard_map/ppermute | solution.py:10
  175.1 13.0 %all-to-all-start.3 = ((bf16[4,128,512]{1,2,0:T(8,128)(2,1)}), bf16[4,128,512]{1,2,0:T(8,128)(2,1)}, u32[]{:S(2)}, u32[]{:S(2)}) async-start(bf16[4,128,512]{1,2,0:T(8,128)(2,1)} %copy.231), calls=%async_computation.3 | async-start | bytes 1048576 | tf_op jit(solution)/shard_map/all_to_all | solution.py:109
  188.1 12.9 %all-to-all-start.7 = ((bf16[4,128,512]{2,1,0:T(8,128)(2,1)}), bf16[4,128,512]{2,1,0:T(8,128)(2,1)S(1)}, u32[]{:S(2)}, u32[]{:S(2)}) async-start(bf16[4,128,512]{2,1,0:T(8,128)(2,1)} %all_to_all.134), calls=%async_computation.7 | async-start | bytes 1048576 | tf_op jit(solution)/shard_map/all_to_all | solution.py:124
  201.0 12.3 %all-to-all-start.6 = ((bf16[4,128,512]{2,1,0:T(8,128)(2,1)}), bf16[4,128,512]{2,1,0:T(8,128)(2,1)S(1)}, u32[]{:S(2)}, u32[]{:S(2)}) async-start(bf16[4,128,512]{2,1,0:T(8,128)(2,1)} %all_to_all.130), calls=%async_computation.6 | async-start | bytes 1048576 | tf_op jit(solution)/shard_map/all_to_all | solution.py:117
where the time goes:
time: 216 us; the launch traced here: 215 us
  waiting for transfers between devices  69.5 us (32%)
  matrix products  52.5 us (24%)
  starting transfers between devices  44.6 us (21%)
  local copies, waits for them, and re-layouts  44 us (20%)
  other arithmetic  2.89 us (1%)
    ppermute x12, waiting for transfers between devices, swapped(): lax.ppermute(x, axis, [(i, i ^ 1 << distance) for i in range(lax.axis_siz...  42.7 us
    unnamed x55, local copies, waits for them, and re-layouts  18.2 us
    dot_general x4, matrix products, block_forward(): jnp.einsum('hqk,khd->qhd', shifted.astype(jnp.bfloat16), value3, preferre...  15.5 us
    ppermute x12, starting transfers between devices, swapped(): lax.ppermute(x, axis, [(i, i ^ 1 << distance) for i in range(lax.axis_siz...  14.7 us
    dot_general x4, matrix products, block_backward(): jnp.einsum('hqk,qhd->khd', score_gradient, query3, preferred_element_type...  9.81 us
    dot_general x4, matrix products, block_forward(): jnp.einsum('qhd,khd->hqk', query3, key3, preferred_element_type=jnp.float32)  8.99 us
    dot_general x4, matrix products, block_backward(): jnp.einsum('hqk,qhd->khd', probs.astype(jnp.bfloat16), grad3, preferred_e...  8.67 us
    all_to_all x1, waiting for transfers between devices, body(): lax.all_to_all(key_rows, 'ulysses', split_axis=1, concat_axis=0, tiled=True)  7.77 us
  transfers between devices with their start and end apart: 20, of which 8 were waited for; matrix products, arithmetic and copies ran while one was open for 31% of the time, Pallas kernels for 0%

commit v1 on v0

--- a/solution.py
+++ b/solution.py
@@ -4,6 +4,29 @@
 from jax.sharding import PartitionSpec as P
 
 HEAD_DIM = 128
+
+
+def split_up(shard, dim, count):
+    shape = shard.shape
+    parts = shard.reshape(*shape[:dim], count, shape[dim] // count, *shape[dim + 1 :])
+    return jnp.moveaxis(parts, dim, 0)
+
+
+def laid_out(tiles, dim):
+    shape = list(tiles.shape[1:])
+    shape[dim] *= tiles.shape[0]
+    return jnp.moveaxis(tiles, 0, dim).reshape(shape)
+
+
+def pairwise_exchange(x, axis, split_dim, concat_dim):
+    size, place = (lax.axis_size(axis), lax.axis_index(axis))
+    pieces = split_up(x, split_dim, size)
+    outs = [pieces[place]]
+    for hop in range(1, size):
+        sent = pieces[place ^ hop]
+        outs.append(lax.ppermute(sent, axis, [(i, i ^ hop) for i in range(size)]))
+    pieces = jnp.stack(outs)[place ^ jnp.arange(size)]
+    return laid_out(pieces, concat_dim)
 
 
 def swapped(x, axis, distance):
@@ -70,7 +93,7 @@
 def body(queries, key_rows, value_rows, grad_out):
     levels = lax.axis_size("context").bit_length() - 1
     query_flat, key_flat, value_flat, grad_flat = (
-        lax.all_to_all(queries, "ulysses", split_axis=1, concat_axis=0, tiled=True),
+        pairwise_exchange(queries, "ulysses", 1, 0),
         lax.all_to_all(key_rows, "ulysses", split_axis=1, concat_axis=0, tiled=True),
         lax.all_to_all(value_rows, "ulysses", split_axis=1, concat_axis=0, tiled=True),
         lax.all_to_all(grad_out, "ulysses", split_axis=1, concat_axis=0, tiled=True),

time: 216 us -> 205 us (0.949)
  waiting for transfers between devices: 69.5 us -> 64 us
  local copies, waits for them, and re-layouts: 44 us -> 41 us
    all_to_all x1 -> x0, waiting for transfers between devices: 6.77 us -> none  [body(): lax.all_to_all(queries, 'ulysses', split_axis=1, concat_axis=0, tiled=True)]
    ppermute x12, waiting for transfers between devices: 42.7 us -> 47.8 us  [swapped(): lax.ppermute(x, axis, [(i, i ^ 1 << distance) for i in range(lax.axis_siz...]
    all_to_all x1 -> x0, starting transfers between devices: 4.24 us -> none  [body(): lax.all_to_all(queries, 'ulysses', split_axis=1, concat_axis=0, tiled=True)]
    all_to_all x1, waiting for transfers between devices: 5.29 us -> 2.69 us  [body(): lax.all_to_all(value_rows, 'ulysses', split_axis=1, concat_axis=0, tiled=...]
    ppermute x0 -> x3, starting transfers between devices: none -> 2.29 us  [pairwise_exchange(): outs.append(lax.ppermute(sent, axis, [(i, i ^ hop) for i in range(size)]))]
    unnamed x55 -> x66, local copies, waits for them, and re-layouts: 18.2 us -> 19.1 us
  transfers between devices with their start and end apart: 20 -> 22, of which waited for: 8 -> 8; matrix products, arithmetic and copies ran while one was open for 31% -> 31% of each run, Pallas kernels for 0% -> 0%
where the time goes in v1:
time: 205 us; the launch traced here: 204 us
  waiting for transfers between devices  64 us (31%)
  matrix products  50.4 us (25%)
  starting transfers between devices  44.2 us (22%)
  local copies, waits for them, and re-layouts  41 us (20%)
  other arithmetic  2.96 us (1%)
    ppermute x12, waiting for transfers between devices, swapped(): lax.ppermute(x, axis, [(i, i ^ 1 << distance) for i in range(lax.axis_siz...  47.8 us
    unnamed x66, local copies, waits for them, and re-layouts  19.1 us
    ppermute x12, starting transfers between devices, swapped(): lax.ppermute(x, axis, [(i, i ^ 1 << distance) for i in range(lax.axis_siz...  14.8 us
    dot_general x4, matrix products, block_forward(): jnp.einsum('hqk,khd->qhd', shifted.astype(jnp.bfloat16), value3, preferre...  14.4 us
    dot_general x4, matrix products, block_forward(): jnp.einsum('qhd,khd->hqk', query3, key3, preferred_element_type=jnp.float32)  8.93 us
    dot_general x4, matrix products, block_backward(): jnp.einsum('hqk,qhd->khd', probs.astype(jnp.bfloat16), grad3, preferred_e...  8.81 us
    dot_general x4, matrix products, block_backward(): jnp.einsum('hqk,qhd->khd', score_gradient, query3, preferred_element_type...  8.67 us
    ppermute x6, local copies, waits for them, and re-layouts, swapped(): lax.ppermute(x, axis, [(i, i ^ 1 << distance) for i in range(lax.axis_siz...  7.52 us
  transfers between devices with their start and end apart: 22, of which 8 were waited for; matrix products, arithmetic and copies ran while one was open for 31% of the time, Pallas kernels for 0%

profile of v1, /device:TPU:0, one launch (start us, length us, event | category | flops | bytes accessed | tf_op | source)
XLA Modules:
  0.0 203.8 jit_solution(15493550092184907213)
XLA Ops:
  0.7 2.1 %copy.236 = bf16[128,2048]{0,1:T(8,128)(2,1)} copy(bf16[128,2048]{1,0:T(8,128)(2,1)} %param.5) | data formatting | bytes 1048576 | tf_op args[1]
  2.8 4.2 %all-to-all-start = ((bf16[128,4,512]{0,2,1:T(8,128)(2,1)}), bf16[128,4,512]{0,2,1:T(8,128)(2,1)S(1)}, u32[]{:S(2)}, u32[]{:S(2)}) async-start(bf16[128,4,512]{0,2,1:T(8,128)(2,1)} %bitcast.9), calls=%async_computation | async-start | bytes 1048576 | tf_op jit(solution)/shard_map/all_to_all | solution.py:97
  7.0 2.0 %copy.240 = bf16[128,2048]{0,1:T(8,128)(2,1)} copy(bf16[128,2048]{1,0:T(8,128)(2,1)} %param.6) | data formatting | bytes 1048576 | tf_op args[2]
  9.1 6.8 %all-to-all-done = bf16[128,4,512]{0,2,1:T(8,128)(2,1)S(1)} async-done(((bf16[128,4,512]{0,2,1:T(8,128)(2,1)}), bf16[128,4,512]{0,2,1:T(8,128)(2,1)S(1)}, u32[]{:S(2)}, u32[]{:S(2)}) %all-to-all-start) | async-done | bytes 524320 | tf_op jit(solution)/shard_map/all_to_all | solution.py:97
  15.8 3.5 %all-to-all-start.1 = ((bf16[128,4,512]{0,2,1:T(8,128)(2,1)}), bf16[128,4,512]{0,2,1:T(8,128)(2,1)S(1)}, u32[]{:S(2)}, u32[]{:S(2)}) async-start(bf16[128,4,512]{0,2,1:T(8,128)(2,1)} %bitcast.11), calls=%async_computation.1 | async-start | bytes 1048576 | tf_op jit(solution)/shard_map/all_to_all | solution.py:98
  20.4 1.7 collective-permute-start.1
  22.6 2.3 %collective-permute-start.3 = (bf16[512,512]{1,0:T(8,128)(2,1)S(1)}, bf16[512,512]{1,0:T(8,128)(2,1)}, u32[]{:S(2)}, u32[]{:S(2)}) collective-permute-start(bf16[512,512]{1,0:T(8,128)(2,1)S(1)} %bitcast.211), channel_id=1, source_target_pairs={{0,1},{1,0},{2,3},{3,2},{4,5},{5,4},{6,7},{7,6},{8,9},{9,8},{10,11... | collective-permute-start | bytes 1572872 | tf_op jit(solution)/shard_map/ppermute | solution.py:33
  25.0 1.0 copy.261
  26.0 2.7 %all-to-all-done.1 = bf16[128,4,512]{0,2,1:T(8,128)(2,1)S(1)} async-done(((bf16[128,4,512]{0,2,1:T(8,128)(2,1)}), bf16[128,4,512]{0,2,1:T(8,128)(2,1)S(1)}, u32[]{:S(2)}, u32[]{:S(2)}) %all-to-all-start.1) | async-done | bytes 524320 | tf_op jit(solution)/shard_map/all_to_all | solution.py:98
  28.7 3.5 %all-to-all-start.3 = ((bf16[128,4,512]{0,2,1:T(8,128)(2,1)}), bf16[128,4,512]{0,2,1:T(8,128)(2,1)S(1)}, u32[]{:S(2)}, u32[]{:S(2)}) async-start(bf16[128,4,512]{0,2,1:T(8,128)(2,1)} %bitcast.37), calls=%async_computation.3 | async-start | bytes 1048576 | tf_op jit(solution)/shard_map/all_to_all | solution.py:99
  34.4 1.0 copy.241
  35.4 3.3 %collective-permute-start.8 = (bf16[512,512]{1,0:T(8,128)(2,1)}, bf16[512,512]{1,0:T(8,128)(2,1)}, u32[]{:S(2)}, u32[]{:S(2)}) collective-permute-start(bf16[512,512]{1,0:T(8,128)(2,1)} %bitcast.19), channel_id=1, source_target_pairs={{0,4},{1,5},{2,6},{3,7},{4,0},{5,1},{6,2},{7,3},{8,12},{9,13},{10,... | collective-permute-start | bytes 1572872 | tf_op jit(solution)/shard_map/ppermute | solution.py:33
  38.7 1.6 collective-permute-start.6
  40.2 1.5 collective-permute-start.4
  42.2 2.7 %multiply_reduce_fusion.3 = (f32[4,512]{1,0:T(4,128)S(1)}, f32[4,512,512]{1,2,0:T(8,128)}) fusion(bf16[512,4,128]{0,2,1:T(8,128)(2,1)S(1)} %copy.285, bf16[512,4,128]{2,1,0:T(4,128)(2,1)S(1)} %reshape.154), kind=kOutput, calls=%fused_computation.28 | convolution fusion | flops 270530560 | bytes 5251072 | tf_op jit(solution)/shard_map/qhd,khd->hqk/dot_general | solution.py:47
  46.6 1.3 copy.245
  47.8 2.8 %multiply_reduce_fusion.2 = (f32[4,512]{1,0:T(4,128)S(1)}, f32[4,512,512]{1,2,0:T(8,128)}) fusion(bf16[512,4,128]{0,2,1:T(8,128)(2,1)S(1)} %copy.285, bf16[512,4,128]{0,2,1:T(8,128)(2,1)S(1)} %bitcast.198), kind=kOutput, calls=%fused_computation.27 | convolution fusion | flops 270530560 | bytes 5251072 | tf_op jit(solution)/shard_map/qhd,khd->hqk/dot_general | solution.py:47
  50.6 35.1 %collective-permute-done.5 = bf16[512,512]{1,0:T(8,128)(2,1)} collective-permute-done((bf16[512,512]{1,0:T(8,128)(2,1)S(1)}, bf16[512,512]{1,0:T(8,128)(2,1)}, u32[]{:S(2)}, u32[]{:S(2)}) %collective-permute-start.5) | collective-permute-done | bytes 524320 | tf_op jit(solution)/shard_map/ppermute | solution.py:33
  85.8 1.3 copy.250
  87.0 2.7 %multiply_reduce_fusion.1 = (f32[4,512]{1,0:T(4,128)S(1)}, f32[4,512,512]{1,2,0:T(8,128)}) fusion(bf16[512,4,128]{0,2,1:T(8,128)(2,1)S(1)} %copy.285, bf16[512,4,128]{0,2,1:T(8,128)(2,1)S(1)} %bitcast.200), kind=kOutput, calls=%fused_computation.26 | convolution fusion | flops 270530560 | bytes 5251072 | tf_op jit(solution)/shard_map/qhd,khd->hqk/dot_general | solution.py:47
  89.7 1.3 copy.255
  91.8 3.1 %copy-done.2 = f32[4,512,512]{1,2,0:T(8,128)S(1)} copy-done((f32[4,512,512]{1,2,0:T(8,128)S(1)}, f32[4,512,512]{1,2,0:T(8,128)}, u32[]{:S(2)}) %copy-start.2) | copy-done | bytes 4194328
  94.9 1.4 fusion.4
  97.1 1.3 copy-done.8
  98.4 1.4 fusion
  99.8 1.6 fusion.121
  102.4 1.3 copy.253
  103.7 4.3 %fusion.74 = f32[512,4,128]{0,2,1:T(8,128)} fusion(bf16[512,4,128]{0,2,1:T(8,128)(2,1)S(1)} %bitcast.204, f32[4,512,512]{1,2,0:T(8,128)} %get-tuple-element.30, f32[4,512]{1,0:T(4,128)S(1)} %get-tuple-element.29, f32[512,4]{0,1:T(4,128)S(1)} %get-tuple-element.21), kind=kOutput, calls=%fused_computation.63 | convolution fusion | flops 271843328 | bytes 5783552 | tf_op jit(solution)/shard_map/hqk,khd->qhd/dot_general | solution.py:52
  108.1 1.8 fusion.118
  109.9 1.6 fusion.115
  111.5 1.3 copy.258
  112.8 4.3 %fusion.80 = f32[512,4,128]{0,2,1:T(8,128)} fusion(bf16[512,4,128]{0,2,1:T(8,128)(2,1)S(1)} %bitcast.206, f32[4,512,512]{1,2,0:T(8,128)} %copy-done.5, f32[4,512]{1,0:T(4,128)S(1)} %get-tuple-element.27, f32[512,4]{0,1:T(4,128)S(1)} %get-tuple-element.22), kind=kOutput, calls=%fused_computation.65 | convolution fusion | flops 271843328 | bytes 5783552 | tf_op jit(solution)/shard_map/hqk,khd->qhd/dot_general | solution.py:52
  117.0 1.3 copy.248
  118.3 4.9 %multiply_reduce_fusion.4 = (f32[512,4]{0,1:T(4,128)S(1)}, bf16[512,4,128]{0,2,1:T(8,128)(2,1)}) fusion(bf16[512,4,128]{0,2,1:T(8,128)(2,1)S(1)} %reshape.162, f32[512,4]{0,1:T(4,128)S(1)} %get-tuple-element.16, f32[512,4,128]{0,2,1:T(8,128)} %fusion.80, f32[512,4]{0,1:T(4,128)S(1)} %get-tuple-element.19, f32[512,4,128]{0,2,1:T(8,128)} %fusion.74, ...), kind=kOutput, calls=%fused_computation.99 | convolution fusion | flops 274724864 | bytes 8962048 | tf_op jit(solution)/shard_map/hqk,khd->qhd/dot_general | solution.py:52
  123.2 1.4 multiply_convert_fusion.2
  125.5 1.4 multiply_convert_fusion.1
  126.9 1.5 copy-done.7
  128.6 1.4 multiply_convert_fusion
  130.9 1.4 multiply_convert_fusion.3
  132.3 1.6 fusion.114
  135.6 2.6 %collective-permute-start.13 = (bf16[512,4,128]{2,0,1:T(8,128)(2,1)}, bf16[512,4,128]{2,0,1:T(8,128)(2,1)}, u32[]{:S(2)}, u32[]{:S(2)}) collective-permute-start(bf16[512,4,128]{2,0,1:T(8,128)(2,1)} %fusion.118), channel_id=1, source_target_pairs={{0,2},{1,3},{2,0},{3,1},{4,6},{5,7},{6,4},{7,5},{8,10},{9,11},{10,... | collective-permute-start | bytes 1572872 | tf_op jit(solution)/shard_map/ppermute | solution.py:33
  138.2 1.5 collective-permute-start.12
  141.6 1.1 fusion.111
  142.7 1.2 copy.283
  143.9 2.0 all_to_all.111
  145.9 4.1 %all-to-all-start.4 = ((bf16[4,128,512]{2,1,0:T(8,128)(2,1)}), bf16[4,128,512]{2,1,0:T(8,128)(2,1)}, u32[]{:S(2)}, u32[]{:S(2)}) async-start(bf16[4,128,512]{2,1,0:T(8,128)(2,1)} %all_to_all.111), calls=%async_computation.4 | async-start | bytes 1048576 | tf_op jit(solution)/shard_map/all_to_all | solution.py:133
  150.1 3.2 %fusion.112 = bf16[512,4,128]{0,2,1:T(8,128)(2,1)} fusion(bf16[512,4,128]{0,2,1:T(8,128)(2,1)S(1)} %copy.285, bf16[4,512,512]{1,2,0:T(8,128)(2,1)} %copy-done.10), kind=kOutput, calls=%fused_computation.91 | convolution fusion | flops 268697600 | bytes 3145728 | tf_op jit(solution)/shard_map/hqk,qhd->khd/dot_general | solution.py:87
  153.8 1.6 fusion.113
  155.4 5.6 %collective-permute-done.14 = bf16[512,4,128]{2,0,1:T(8,128)(2,1)} collective-permute-done((bf16[512,4,128]{2,0,1:T(8,128)(2,1)}, bf16[512,4,128]{2,0,1:T(8,128)(2,1)}, u32[]{:S(2)}, u32[]{:S(2)}) %collective-permute-start.14) | collective-permute-done | bytes 524320 | tf_op jit(solution)/shard_map/ppermute | solution.py:33
  161.0 1.2 all_to_all.104
  163.0 4.2 %all-to-all-start.2 = ((bf16[4,128,512]{1,2,0:T(8,128)(2,1)}), bf16[4,128,512]{1,2,0:T(8,128)(2,1)}, u32[]{:S(2)}, u32[]{:S(2)}) async-start(bf16[4,128,512]{1,2,0:T(8,128)(2,1)} %copy.260), calls=%async_computation.2 | async-start | bytes 1048576 | tf_op jit(solution)/shard_map/all_to_all | solution.py:132
  167.2 3.8 %add_convert_fusion = bf16[512,4,128]{2,0,1:T(8,128)(2,1)S(1)} fusion(bf16[512,4,128]{2,0,1:T(8,128)(2,1)} %collective-permute-done.14, bf16[512,4,128]{2,0,1:T(8,128)(2,1)} %collective-permute-done.13, bf16[512,4,128]{2,0,1:T(8,128)(2,1)} %collective-permute-done.12, bf16[512,4,128]{0,2,1:T(8,128)(2,1)S(1)} %reshape.162, ...), kind=kOutput, calls=%fused_computation.97 | convolution fusion | flops 273940480 | bytes 6823936 | tf_op jit(solution)/shard_map/hqk,qhd->khd/dot_general | solution.py:75
  172.4 3.7 %all-to-all-done.2 = bf16[4,128,512]{1,2,0:T(8,128)(2,1)} async-done(((bf16[4,128,512]{1,2,0:T(8,128)(2,1)}), bf16[4,128,512]{1,2,0:T(8,128)(2,1)}, u32[]{:S(2)}, u32[]{:S(2)}) %all-to-all-start.2) | async-done | bytes 524320 | tf_op jit(solution)/shard_map/all_to_all | solution.py:132
  176.1 4.1 %all-to-all-start.6 = ((bf16[4,128,512]{2,1,0:T(8,128)(2,1)}), bf16[4,128,512]{2,1,0:T(8,128)(2,1)}, u32[]{:S(2)}, u32[]{:S(2)}) async-start(bf16[4,128,512]{2,1,0:T(8,128)(2,1)} %all_to_all.119), calls=%async_computation.6 | async-start | bytes 1048576 | tf_op jit(solution)/shard_map/all_to_all | solution.py:147
  180.2 7.0 %collective-permute-done.11 = bf16[512,4,128]{0,2,1:T(8,128)(2,1)} collective-permute-done((bf16[512,4,128]{0,2,1:T(8,128)(2,1)}, bf16[512,4,128]{0,2,1:T(8,128)(2,1)}, u32[]{:S(2)}, u32[]{:S(2)}) %collective-permute-start.11) | collective-permute-done | bytes 524320 | tf_op jit(solution)/shard_map/ppermute | solution.py:33
  187.3 2.2 %add_convert_fusion.1 = bf16[512,4,128]{0,2,1:T(8,128)(2,1)S(1)} fusion(bf16[512,4,128]{0,2,1:T(8,128)(2,1)} %collective-permute-done.11, bf16[512,4,128]{0,2,1:T(8,128)(2,1)} %collective-permute-done.10, bf16[512,4,128]{0,2,1:T(8,128)(2,1)} %collective-permute-done.9, bf16[512,4,128]{0,2,1:T(8,128)(2,1)S(1)} %copy.285, bf16[4,512,512]{1,2,0:T(8,128)(2,1)S(1)} %copy-done.12), kind=kOutput, calls=%fused_computation.98 | convolution fusion | flops 270794752 | bytes 4718592 | tf_op jit(solution)/shard_map/hqk,qhd->khd/dot_general | solution.py:87
  190.5 3.5 %all-to-all-start.5 = ((bf16[4,128,512]{1,2,0:T(8,128)(2,1)}), bf16[4,128,512]{1,2,0:T(8,128)(2,1)S(1)}, u32[]{:S(2)}, u32[]{:S(2)}) async-start(bf16[4,128,512]{1,2,0:T(8,128)(2,1)} %copy.293), calls=%async_computation.5 | async-start | bytes 1048576 | tf_op jit(solution)/shard_map/all_to_all | solution.py:140
  194.0 1.3 copy.284
  195.3 1.0 copy.301
  196.3 2.0 %copy.300 = bf16[128,2048]{1,0:T(8,128)(2,1)} copy(bf16[128,2048]{0,1:T(8,128)(2,1)} %bitcast.36) | data formatting | bytes 1048576
  198.4 1.3 copy.299
  199.7 1.0 copy.303
  200.7 2.1 %all-to-all-done.5 = bf16[4,128,512]{1,2,0:T(8,128)(2,1)S(1)} async-done(((bf16[4,128,512]{1,2,0:T(8,128)(2,1)}), bf16[4,128,512]{1,2,0:T(8,128)(2,1)S(1)}, u32[]{:S(2)}, u32[]{:S(2)}) %all-to-all-start.5) | async-done | bytes 524320 | tf_op jit(solution)/shard_map/all_to_all | solution.py:140
  202.8 1.0 copy.302
  (108 shorter events, 17.5 us)
Async XLA Ops:
  0.6 18.7 %copy-start.27 = (bf16[128,2048]{1,0:T(8,128)(2,1)S(1)}, bf16[128,2048]{1,0:T(8,128)(2,1)}, u32[]{:S(2)}) copy-start(bf16[128,2048]{1,0:T(8,128)(2,1)} %param.4) | copy-start | bytes 1572868
  0.6 24.3 %copy-start.28 = (bf16[128,2048]{1,0:T(8,128)(2,1)S(1)}, bf16[128,2048]{1,0:T(8,128)(2,1)}, u32[]{:S(2)}) copy-start(bf16[128,2048]{1,0:T(8,128)(2,1)} %param.7) | copy-start | bytes 1572868
  2.8 13.1 %all-to-all-start = ((bf16[128,4,512]{0,2,1:T(8,128)(2,1)}), bf16[128,4,512]{0,2,1:T(8,128)(2,1)S(1)}, u32[]{:S(2)}, u32[]{:S(2)}) async-start(bf16[128,4,512]{0,2,1:T(8,128)(2,1)} %bitcast.9), calls=%async_computation | async-start | bytes 1048576 | tf_op jit(solution)/shard_map/all_to_all | solution.py:97
  15.8 12.8 %all-to-all-start.1 = ((bf16[128,4,512]{0,2,1:T(8,128)(2,1)}), bf16[128,4,512]{0,2,1:T(8,128)(2,1)S(1)}, u32[]{:S(2)}, u32[]{:S(2)}) async-start(bf16[128,4,512]{0,2,1:T(8,128)(2,1)} %bitcast.11), calls=%async_computation.1 | async-start | bytes 1048576 | tf_op jit(solution)/shard_map/all_to_all | solution.py:98
  19.8 12.3 %collective-permute-start = (bf16[128,512]{1,0:T(8,128)(2,1)S(1)}, bf16[128,512]{1,0:T(8,128)(2,1)S(1)}, u32[]{:S(2)}, u32[]{:S(2)}) collective-permute-start(bf16[128,512]{1,0:T(8,128)(2,1)S(1)} %bitcast.225), channel_id=1, source_target_pairs={{0,8},{8,0},{16,24},{24,16},{1,9},{9,1},{17,25},{25,17},{2,10},{10... | collective-permute-start | bytes 393224 | tf_op jit(solution)/shard_map/ppermute | solution.py:27
  20.4 11.7 %collective-permute-start.1 = (bf16[128,512]{1,0:T(8,128)(2,1)S(1)}, bf16[128,512]{1,0:T(8,128)(2,1)S(1)}, u32[]{:S(2)}, u32[]{:S(2)}) collective-permute-start(bf16[128,512]{1,0:T(8,128)(2,1)S(1)} %bitcast.226), channel_id=1, source_target_pairs={{0,16},{8,24},{16,0},{24,8},{1,17},{9,25},{17,1},{25,9},{2,18},{10... | collective-permute-start | bytes 393224 | tf_op jit(solution)/shard_map/ppermute | solution.py:27
  22.3 10.9 %collective-permute-start.2 = (bf16[128,512]{1,0:T(8,128)(2,1)S(1)}, bf16[128,512]{1,0:T(8,128)(2,1)S(1)}, u32[]{:S(2)}, u32[]{:S(2)}) collective-permute-start(bf16[128,512]{1,0:T(8,128)(2,1)S(1)} %bitcast.227), channel_id=1, source_target_pairs={{0,24},{8,16},{16,8},{24,0},{1,25},{9,17},{17,9},{25,1},{2,26},{10... | collective-permute-start | bytes 393224 | tf_op jit(solution)/shard_map/ppermute | solution.py:27
  22.6 23.6 %collective-permute-start.3 = (bf16[512,512]{1,0:T(8,128)(2,1)S(1)}, bf16[512,512]{1,0:T(8,128)(2,1)}, u32[]{:S(2)}, u32[]{:S(2)}) collective-permute-start(bf16[512,512]{1,0:T(8,128)(2,1)S(1)} %bitcast.211), channel_id=1, source_target_pairs={{0,1},{1,0},{2,3},{3,2},{4,5},{5,4},{6,7},{7,6},{8,9},{9,8},{10,11... | collective-permute-start | bytes 1572872 | tf_op jit(solution)/shard_map/ppermute | solution.py:33
  28.7 16.9 %all-to-all-start.3 = ((bf16[128,4,512]{0,2,1:T(8,128)(2,1)}), bf16[128,4,512]{0,2,1:T(8,128)(2,1)S(1)}, u32[]{:S(2)}, u32[]{:S(2)}) async-start(bf16[128,4,512]{0,2,1:T(8,128)(2,1)} %bitcast.37), calls=%async_computation.3 | async-start | bytes 1048576 | tf_op jit(solution)/shard_map/all_to_all | solution.py:99
  34.4 11.1 %copy-start.13 = (bf16[512,4,128]{2,1,0:T(4,128)(2,1)}, bf16[512,4,128]{2,1,0:T(4,128)(2,1)S(1)}, u32[]{:S(2)}) copy-start(bf16[512,4,128]{2,1,0:T(4,128)(2,1)S(1)} %reshape.154) | copy-start | bytes 1572868
  35.4 76.1 %collective-permute-start.8 = (bf16[512,512]{1,0:T(8,128)(2,1)}, bf16[512,512]{1,0:T(8,128)(2,1)}, u32[]{:S(2)}, u32[]{:S(2)}) collective-permute-start(bf16[512,512]{1,0:T(8,128)(2,1)} %bitcast.19), channel_id=1, source_target_pairs={{0,4},{1,5},{2,6},{3,7},{4,0},{5,1},{6,2},{7,3},{8,12},{9,13},{10,... | collective-permute-start | bytes 1572872 | tf_op jit(solution)/shard_map/ppermute | solution.py:33
  38.7 63.8 %collective-permute-start.6 = (bf16[512,512]{1,0:T(8,128)(2,1)}, bf16[512,512]{1,0:T(8,128)(2,1)}, u32[]{:S(2)}, u32[]{:S(2)}) collective-permute-start(bf16[512,512]{1,0:T(8,128)(2,1)} %bitcast.19), channel_id=1, source_target_pairs={{0,2},{1,3},{2,0},{3,1},{4,6},{5,7},{6,4},{7,5},{8,10},{9,11},{10,... | collective-permute-start | bytes 1572872 | tf_op jit(solution)/shard_map/ppermute | solution.py:33
  40.2 76.8 %collective-permute-start.4 = (bf16[512,512]{1,0:T(8,128)(2,1)}, bf16[512,512]{1,0:T(8,128)(2,1)}, u32[]{:S(2)}, u32[]{:S(2)}) collective-permute-start(bf16[512,512]{1,0:T(8,128)(2,1)} %bitcast.19), channel_id=1, source_target_pairs={{0,1},{1,0},{2,3},{3,2},{4,5},{5,4},{6,7},{7,6},{8,9},{9,8},{10,11... | collective-permute-start | bytes 1572872 | tf_op jit(solution)/shard_map/ppermute | solution.py:33
  41.8 44.0 %collective-permute-start.5 = (bf16[512,512]{1,0:T(8,128)(2,1)S(1)}, bf16[512,512]{1,0:T(8,128)(2,1)}, u32[]{:S(2)}, u32[]{:S(2)}) collective-permute-start(bf16[512,512]{1,0:T(8,128)(2,1)S(1)} %bitcast.212), channel_id=1, source_target_pairs={{0,2},{1,3},{2,0},{3,1},{4,6},{5,7},{6,4},{7,5},{8,10},{9,11},{10,... | collective-permute-start | bytes 1572872 | tf_op jit(solution)/shard_map/ppermute | solution.py:33
  45.5 56.0 %copy-start.17 = (bf16[512,4,128]{0,2,1:T(8,128)(2,1)}, bf16[512,4,128]{0,2,1:T(8,128)(2,1)S(1)}, u32[]{:S(2)}) copy-start(bf16[512,4,128]{0,2,1:T(8,128)(2,1)S(1)} %reshape.155) | copy-start | bytes 1572868
  46.2 43.6 %collective-permute-start.7 = (bf16[512,512]{1,0:T(8,128)(2,1)S(1)}, bf16[512,512]{1,0:T(8,128)(2,1)}, u32[]{:S(2)}, u32[]{:S(2)}) collective-permute-start(bf16[512,512]{1,0:T(8,128)(2,1)S(1)} %bitcast.213), channel_id=1, source_target_pairs={{0,4},{1,5},{2,6},{3,7},{4,0},{5,1},{6,2},{7,3},{8,12},{9,13},{10,... | collective-permute-start | bytes 1572872 | tf_op jit(solution)/shard_map/ppermute | solution.py:33
  47.8 41.9 %copy-start.15 = (bf16[512,512]{0,1:T(8,128)(2,1)}, bf16[512,512]{0,1:T(8,128)(2,1)S(1)}, u32[]{:S(2)}) copy-start(bf16[512,512]{0,1:T(8,128)(2,1)S(1)} %copy.245) | copy-start | bytes 1572868
  87.0 4.8 %copy-start.19 = (bf16[512,512]{0,1:T(8,128)(2,1)}, bf16[512,512]{0,1:T(8,128)(2,1)S(1)}, u32[]{:S(2)}) copy-start(bf16[512,512]{0,1:T(8,128)(2,1)S(1)} %copy.250) | copy-start | bytes 1572868
  91.0 5.3 %copy-start.21 = (bf16[512,512]{0,1:T(8,128)(2,1)}, bf16[512,512]{0,1:T(8,128)(2,1)S(1)}, u32[]{:S(2)}) copy-start(bf16[512,512]{0,1:T(8,128)(2,1)S(1)} %copy.255) | copy-start | bytes 1572868
  91.0 3.9 %copy-start.2 = (f32[4,512,512]{1,2,0:T(8,128)S(1)}, f32[4,512,512]{1,2,0:T(8,128)}, u32[]{:S(2)}) copy-start(f32[4,512,512]{1,2,0:T(8,128)} %get-tuple-element.30) | copy-start | bytes 12582916
  91.8 4.5 %copy-start.5 = (f32[4,512,512]{1,2,0:T(8,128)}, f32[4,512,512]{1,2,0:T(8,128)S(1)}, u32[]{:S(2)}) copy-start(f32[4,512,512]{1,2,0:T(8,128)S(1)} %get-tuple-element.28) | copy-start | bytes 12582916
  94.9 2.2 %copy-start = (f32[4,512,512]{1,2,0:T(8,128)S(1)}, f32[4,512,512]{1,2,0:T(8,128)}, u32[]{:S(2)}) copy-start(f32[4,512,512]{1,2,0:T(8,128)} %get-tuple-element.34) | copy-start | bytes 12582916
  94.9 3.5 %copy-start.8 = (f32[4,512,512]{1,2,0:T(8,128)S(1)}, f32[4,512,512]{1,2,0:T(8,128)}, u32[]{:S(2)}) copy-start(f32[4,512,512]{1,2,0:T(8,128)} %get-tuple-element.32) | copy-start | bytes 12582916
  103.7 6.2 %copy-start.23 = (bf16[512,512]{0,1:T(8,128)(2,1)}, bf16[512,512]{0,1:T(8,128)(2,1)S(1)}, u32[]{:S(2)}) copy-start(bf16[512,512]{0,1:T(8,128)(2,1)S(1)} %copy.253) | copy-start | bytes 1572868
  103.7 4.3 %copy-start.3 = (f32[4,512,512]{1,2,0:T(8,128)S(1)}, f32[4,512,512]{1,2,0:T(8,128)}, u32[]{:S(2)}) copy-start(f32[4,512,512]{1,2,0:T(8,128)} %get-tuple-element.30) | copy-start | bytes 12582916
  103.7 6.2 %copy-start.6 = (f32[4,512,512]{1,2,0:T(8,128)S(1)}, f32[4,512,512]{1,2,0:T(8,128)}, u32[]{:S(2)}) copy-start(f32[4,512,512]{1,2,0:T(8,128)} %copy-done.5) | copy-start | bytes 12582916
  112.7 10.5 %copy-start.25 = (bf16[512,512]{0,1:T(8,128)(2,1)}, bf16[512,512]{0,1:T(8,128)(2,1)S(1)}, u32[]{:S(2)}) copy-start(bf16[512,512]{0,1:T(8,128)(2,1)S(1)} %copy.258) | copy-start | bytes 1572868
  118.3 4.9 %copy-start.9 = (f32[4,512,512]{1,2,0:T(8,128)S(1)}, f32[4,512,512]{1,2,0:T(8,128)}, u32[]{:S(2)}) copy-start(f32[4,512,512]{1,2,0:T(8,128)} %get-tuple-element.32) | copy-start | bytes 12582916
  123.2 2.2 %copy-start.4 = (f32[4,512,512]{1,2,0:T(8,128)S(1)}, f32[4,512,512]{1,2,0:T(8,128)}, u32[]{:S(2)}) copy-start(f32[4,512,512]{1,2,0:T(8,128)} %get-tuple-element.30) | copy-start | bytes 12582916
  123.2 2.3 %copy-start.24 = (bf16[512,512]{0,1:T(8,128)(2,1)S(1)}, bf16[512,512]{0,1:T(8,128)(2,1)}, u32[]{:S(2)}) copy-start(bf16[512,512]{0,1:T(8,128)(2,1)} %copy-done.23) | copy-start | bytes 1572868
  125.5 16.0 %copy-start.10 = (bf16[4,512,512]{1,2,0:T(8,128)(2,1)}, bf16[4,512,512]{1,2,0:T(8,128)(2,1)S(1)}, u32[]{:S(2)}) copy-start(bf16[4,512,512]{1,2,0:T(8,128)(2,1)S(1)} %multiply_convert_fusion.2) | copy-start | bytes 6291460
  125.5 2.9 %copy-start.7 = (f32[4,512,512]{1,2,0:T(8,128)S(1)}, f32[4,512,512]{1,2,0:T(8,128)}, u32[]{:S(2)}) copy-start(f32[4,512,512]{1,2,0:T(8,128)} %copy-done.5) | copy-start | bytes 12582916
  125.5 3.1 %copy-start.26 = (bf16[512,512]{0,1:T(8,128)(2,1)S(1)}, bf16[512,512]{0,1:T(8,128)(2,1)}, u32[]{:S(2)}) copy-start(bf16[512,512]{0,1:T(8,128)(2,1)} %copy-done.25) | copy-start | bytes 1572868
  128.6 2.2 %copy-start.1 = (f32[4,512,512]{1,2,0:T(8,128)S(1)}, f32[4,512,512]{1,2,0:T(8,128)}, u32[]{:S(2)}) copy-start(f32[4,512,512]{1,2,0:T(8,128)} %get-tuple-element.34) | copy-start | bytes 12582916
  128.6 2.3 %copy-start.18 = (bf16[512,4,128]{0,2,1:T(8,128)(2,1)S(1)}, bf16[512,4,128]{0,2,1:T(8,128)(2,1)}, u32[]{:S(2)}) copy-start(bf16[512,4,128]{0,2,1:T(8,128)(2,1)} %copy-done.17) | copy-start | bytes 1572868
  130.9 3.1 %copy-start.22 = (bf16[512,512]{0,1:T(8,128)(2,1)S(1)}, bf16[512,512]{0,1:T(8,128)(2,1)}, u32[]{:S(2)}) copy-start(bf16[512,512]{0,1:T(8,128)(2,1)} %copy-done.21) | copy-start | bytes 1572868
  132.3 8.3 %copy-start.11 = (bf16[4,512,512]{1,2,0:T(8,128)(2,1)}, bf16[4,512,512]{1,2,0:T(8,128)(2,1)S(1)}, u32[]{:S(2)}) copy-start(bf16[4,512,512]{1,2,0:T(8,128)(2,1)S(1)} %multiply_convert_fusion.3) | copy-start | bytes 6291460
  132.3 7.4 %copy-start.14 = (bf16[512,4,128]{2,1,0:T(4,128)(2,1)S(1)}, bf16[512,4,128]{2,1,0:T(4,128)(2,1)}, u32[]{:S(2)}) copy-start(bf16[512,4,128]{2,1,0:T(4,128)(2,1)} %copy-done.13) | copy-start | bytes 1572868
  134.0 6.7 %copy-start.20 = (bf16[512,512]{0,1:T(8,128)(2,1)S(1)}, bf16[512,512]{0,1:T(8,128)(2,1)}, u32[]{:S(2)}) copy-start(bf16[512,512]{0,1:T(8,128)(2,1)} %copy-done.19) | copy-start | bytes 1572868
  134.9 6.7 %copy-start.16 = (bf16[512,512]{0,1:T(8,128)(2,1)S(1)}, bf16[512,512]{0,1:T(8,128)(2,1)}, u32[]{:S(2)}) copy-start(bf16[512,512]{0,1:T(8,128)(2,1)} %copy-done.15) | copy-start | bytes 1572868
  134.9 26.1 %collective-permute-start.14 = (bf16[512,4,128]{2,0,1:T(8,128)(2,1)}, bf16[512,4,128]{2,0,1:T(8,128)(2,1)}, u32[]{:S(2)}, u32[]{:S(2)}) collective-permute-start(bf16[512,4,128]{2,0,1:T(8,128)(2,1)} %fusion.115), channel_id=1, source_target_pairs={{0,4},{1,5},{2,6},{3,7},{4,0},{5,1},{6,2},{7,3},{8,12},{9,13},{10,... | collective-permute-start | bytes 1572872 | tf_op jit(solution)/shard_map/ppermute | solution.py:33
  135.6 31.6 %collective-permute-start.13 = (bf16[512,4,128]{2,0,1:T(8,128)(2,1)}, bf16[512,4,128]{2,0,1:T(8,128)(2,1)}, u32[]{:S(2)}, u32[]{:S(2)}) collective-permute-start(bf16[512,4,128]{2,0,1:T(8,128)(2,1)} %fusion.118), channel_id=1, source_target_pairs={{0,2},{1,3},{2,0},{3,1},{4,6},{5,7},{6,4},{7,5},{8,10},{9,11},{10,... | collective-permute-start | bytes 1572872 | tf_op jit(solution)/shard_map/ppermute | solution.py:33
  138.2 29.1 %collective-permute-start.12 = (bf16[512,4,128]{2,0,1:T(8,128)(2,1)}, bf16[512,4,128]{2,0,1:T(8,128)(2,1)}, u32[]{:S(2)}, u32[]{:S(2)}) collective-permute-start(bf16[512,4,128]{2,0,1:T(8,128)(2,1)} %fusion.121), channel_id=1, source_target_pairs={{0,1},{1,0},{2,3},{3,2},{4,5},{5,4},{6,7},{7,6},{8,9},{9,8},{10,11... | collective-permute-start | bytes 1572872 | tf_op jit(solution)/shard_map/ppermute | solution.py:33
  145.9 17.1 %all-to-all-start.4 = ((bf16[4,128,512]{2,1,0:T(8,128)(2,1)}), bf16[4,128,512]{2,1,0:T(8,128)(2,1)}, u32[]{:S(2)}, u32[]{:S(2)}) async-start(bf16[4,128,512]{2,1,0:T(8,128)(2,1)} %all_to_all.111), calls=%async_computation.4 | async-start | bytes 1048576 | tf_op jit(solution)/shard_map/all_to_all | solution.py:133
  153.3 26.9 %collective-permute-start.9 = (bf16[512,4,128]{0,2,1:T(8,128)(2,1)}, bf16[512,4,128]{0,2,1:T(8,128)(2,1)}, u32[]{:S(2)}, u32[]{:S(2)}) collective-permute-start(bf16[512,4,128]{0,2,1:T(8,128)(2,1)} %fusion.112), channel_id=1, source_target_pairs={{0,1},{1,0},{2,3},{3,2},{4,5},{5,4},{6,7},{7,6},{8,9},{9,8},{10,11... | collective-permute-start | bytes 1572872 | tf_op jit(solution)/shard_map/ppermute | solution.py:33
  155.4 24.8 %collective-permute-start.10 = (bf16[512,4,128]{0,2,1:T(8,128)(2,1)}, bf16[512,4,128]{0,2,1:T(8,128)(2,1)}, u32[]{:S(2)}, u32[]{:S(2)}) collective-permute-start(bf16[512,4,128]{0,2,1:T(8,128)(2,1)} %fusion.113), channel_id=1, source_target_pairs={{0,2},{1,3},{2,0},{3,1},{4,6},{5,7},{6,4},{7,5},{8,10},{9,11},{10,... | collective-permute-start | bytes 1572872 | tf_op jit(solution)/shard_map/ppermute | solution.py:33
  161.0 26.3 %collective-permute-start.11 = (bf16[512,4,128]{0,2,1:T(8,128)(2,1)}, bf16[512,4,128]{0,2,1:T(8,128)(2,1)}, u32[]{:S(2)}, u32[]{:S(2)}) collective-permute-start(bf16[512,4,128]{0,2,1:T(8,128)(2,1)} %fusion.114), channel_id=1, source_target_pairs={{0,4},{1,5},{2,6},{3,7},{4,0},{5,1},{6,2},{7,3},{8,12},{9,13},{10,... | collective-permute-start | bytes 1572872 | tf_op jit(solution)/shard_map/ppermute | solution.py:33
  163.0 13.0 %all-to-all-start.2 = ((bf16[4,128,512]{1,2,0:T(8,128)(2,1)}), bf16[4,128,512]{1,2,0:T(8,128)(2,1)}, u32[]{:S(2)}, u32[]{:S(2)}) async-start(bf16[4,128,512]{1,2,0:T(8,128)(2,1)} %copy.260), calls=%async_computation.2 | async-start | bytes 1048576 | tf_op jit(solution)/shard_map/all_to_all | solution.py:132
  167.2 20.1 %copy-start.12 = (bf16[4,512,512]{1,2,0:T(8,128)(2,1)S(1)}, bf16[4,512,512]{1,2,0:T(8,128)(2,1)}, u32[]{:S(2)}) copy-start(bf16[4,512,512]{1,2,0:T(8,128)(2,1)} %copy-done.11) | copy-start | bytes 6291460
  176.1 14.5 %all-to-all-start.6 = ((bf16[4,128,512]{2,1,0:T(8,128)(2,1)}), bf16[4,128,512]{2,1,0:T(8,128)(2,1)}, u32[]{:S(2)}, u32[]{:S(2)}) async-start(bf16[4,128,512]{2,1,0:T(8,128)(2,1)} %all_to_all.119), calls=%async_computation.6 | async-start | bytes 1048576 | tf_op jit(solution)/shard_map/all_to_all | solution.py:147
  190.5 12.3 %all-to-all-start.5 = ((bf16[4,128,512]{1,2,0:T(8,128)(2,1)}), bf16[4,128,512]{1,2,0:T(8,128)(2,1)S(1)}, u32[]{:S(2)}, u32[]{:S(2)}) async-start(bf16[4,128,512]{1,2,0:T(8,128)(2,1)} %copy.293), calls=%async_computation.5 | async-start | bytes 1048576 | tf_op jit(solution)/shard_map/all_to_all | solution.py:140
